TPU v7x, 32 devices: a whole 2x2x4 slice. The times are simulated.
32 devices in a mesh: row: 8 (over z, y), col: 4 (over x, core).
Axes of the slice: x: 2, y: 2, z: 4, core: 2. Of those that a mesh axis runs over, the one named last changes fastest.
Arguments:
- image: bfloat16 [2048, 512], P(('row', 'col')), may hold values from -2 to 2
- text: bfloat16 [2048, 512], P(('row', 'col')), may hold values from -3 to 3
- logit_scale: float32 [1], replicated, may hold values from 10 to 100
Outputs:
- loss: float32 [1], replicated
- grad_image: float32 [2048, 512], P(('row', 'col'))
- grad_text: float32 [2048, 512], P(('row', 'col'))
All inputs are finite; a program needn't handle non-finite values.
Results may differ from a plain program's by a relative error of at most 0.0095.
Values may be sent and summed in bfloat16 or wider, within the bound.
No kernel may reach another device: no remote copies, remote signals or barrier semaphores. Data moves between devices by JAX's collectives and lax.ppermute only.
A program may use at most 64 MiB of HBM per device.

v0:
```python
import jax
import jax.numpy as jnp
from jax import lax
from jax.sharding import PartitionSpec as P


def normalize(embedding):
    values = embedding.astype(jnp.float32)
    length = jnp.sqrt(jnp.sum(values * values, axis=1, keepdims=True) + 1e-06)
    return (values / length, length)


def unnormalize(unit_rows, length, gradient):
    return (gradient - unit_rows * jnp.sum(unit_rows * gradient, axis=1, keepdims=True)) / length


def on_device(image, text, logit_scale):
    sharpness = logit_scale[0]
    unit_image, image_len = normalize(image)
    unit_text, text_len = normalize(text)
    img_own = unit_image.astype(jnp.bfloat16)
    txt_own = unit_text.astype(jnp.bfloat16)
    img_tile = lax.all_gather(img_own, "col", axis=0, tiled=True)
    txt_tile = lax.all_gather(txt_own, "row", axis=0, tiled=True)
    columns = txt_tile.shape[0]
    block_cols = min(512, columns)
    block_count = columns // block_cols
    txt_blocks = txt_tile.reshape(block_count, block_cols, txt_tile.shape[1])

    def scores(txt_block):
        return sharpness * jnp.einsum(
            "re,ce->rc", img_tile, txt_block, preferred_element_type=jnp.float32
        )

    lowest = jnp.full((img_tile.shape[0],), -1e30, jnp.float32)

    def peaks(running, txt_block):
        logits = scores(txt_block)
        return (jnp.maximum(running, jnp.max(logits, axis=1)), jnp.max(logits, axis=0))

    row_peak, col_peak = lax.scan(peaks, lowest, txt_blocks)
    row_peak = lax.pmax(row_peak, "col")
    col_peak = lax.pmax(col_peak.reshape(-1), "row")

    def sums(running, inputs):
        txt_block, peak_cols = inputs
        logits = scores(txt_block)
        running = running + jnp.sum(jnp.exp(logits - row_peak[:, None]), axis=1)
        return (running, jnp.sum(jnp.exp(logits - peak_cols[None, :]), axis=0))

    row_sum, col_sum = lax.scan(
        sums, jnp.zeros_like(lowest), (txt_blocks, col_peak.reshape(block_count, block_cols))
    )
    row_sum = lax.psum(row_sum, "col")
    col_sum = lax.psum(col_sum.reshape(-1), "row")
    row_lse = row_peak + jnp.log(row_sum)
    col_lse = col_peak + jnp.log(col_sum)
    own_rows = image.shape[0]
    row_mine = lax.dynamic_slice_in_dim(row_lse, lax.axis_index("col") * own_rows, own_rows)
    col_mine = lax.dynamic_slice_in_dim(col_lse, lax.axis_index("row") * own_rows, own_rows)
    img_wide = img_own.astype(jnp.float32)
    txt_wide = txt_own.astype(jnp.float32)
    positive = sharpness * jnp.sum(img_wide * txt_wide, axis=1)
    partial_value = jnp.sum(row_mine - positive) + jnp.sum(col_mine - positive)
    overall = lax.psum(partial_value, ("row", "col"))
    batch_size = own_rows * lax.axis_size("row") * lax.axis_size("col")
    loss = (overall / (2 * batch_size)).reshape(1)

    def weights_of(txt_block, lse_cols):
        logits = scores(txt_block)
        return (
            0.5 * (jnp.exp(logits - row_lse[:, None]) + jnp.exp(logits - lse_cols[None, :]))
        ).astype(jnp.bfloat16)

    start_grad = jnp.zeros((img_tile.shape[0], img_tile.shape[1]), jnp.float32)
    lse_blocks = col_lse.reshape(block_count, block_cols)

    def backward(running, inputs):
        txt_block, lse_cols = inputs
        weights = weights_of(txt_block, lse_cols)
        running = running + sharpness * jnp.dot(
            weights, txt_block, preferred_element_type=jnp.float32
        )
        return (
            running,
            sharpness
            * jnp.einsum("rc,re->ce", weights, img_tile, preferred_element_type=jnp.float32),
        )

    img_terms, txt_terms = lax.scan(backward, start_grad, (txt_blocks, lse_blocks))
    txt_grad = lax.psum_scatter(
        txt_terms.reshape(columns, img_tile.shape[1]), "row", scatter_dimension=0, tiled=True
    )
    img_grad = lax.psum_scatter(img_terms, "col", scatter_dimension=0, tiled=True)
    img_grad = img_grad - sharpness * txt_wide
    txt_grad = txt_grad - sharpness * img_wide
    return (
        loss,
        unnormalize(unit_image, image_len, img_grad),
        unnormalize(unit_text, text_len, txt_grad),
    )


def solution(mesh):
    placed = (P(("row", "col"), None), P(("row", "col"), None), P())
    return jax.shard_map(
        on_device,
        mesh=mesh,
        in_specs=placed,
        out_specs=(P(), P(("row", "col"), None), P(("row", "col"), None)),
        check_vma=False,
    )
```

profile of v0, /device:TPU:0, one launch (start us, length us, event | category | flops | bytes accessed | tf_op | source)
XLA Modules:
  0.0 241.8 jit_solution(7064855430679958634)
XLA Ops:
  7.2 0.0 copy-start.1
  7.2 0.0 reduce-scatter.3.cloned.1.call-start
  7.9 1.0 fusion.1
  8.8 0.0 copy-done.1
  8.8 0.1 fusion.6
  8.9 0.0 copy-start
  9.0 33.2 %all_gather.7 = bf16[512,512]{1,0:T(8,128)(2,1)S(1)} all-gather(bf16[64,512]{1,0:T(8,128)(2,1)S(1)} %fusion.6), channel_id=1, replica_groups=mesh['row'=8,'col'=4] {'row'}, dimensions={0}, use_global_device_ids=true | all-gather | bytes 589824 | tf_op jit(solution)/shard_map/all_gather | solution.py:24
  42.1 0.0 copy-done
  42.1 0.1 fusion
  42.2 0.1 fusion.5
  42.3 5.8 %all_gather.6 = bf16[256,512]{1,0:T(8,128)(2,1)S(1)} all-gather(bf16[64,512]{1,0:T(8,128)(2,1)S(1)} %fusion.5), channel_id=1, replica_groups=mesh['row'=8,'col'=4] {'col'}, dimensions={0}, use_global_device_ids=true | all-gather | bytes 327680 | tf_op jit(solution)/shard_map/all_gather | solution.py:23
  48.1 0.4 fusion.7
  48.6 7.1 %pmax.14 = f32[256]{0:T(256)S(1)} all-reduce(f32[256]{0:T(256)S(1)} %broadcast_maximum_fusion), channel_id=1, replica_groups=mesh['row'=8,'col'=4] {'col'}, use_global_device_ids=true, to_apply=%region_3.0 | all-reduce | flops 256 | bytes 2048 | tf_op jit(solution)/shard_map/pmax | solution.py:42
  55.6 21.5 %pmax.15 = f32[512]{0:T(512)S(1)} all-reduce(f32[512]{0:T(512)S(1)} %get-tuple-element.47), channel_id=1, replica_groups=mesh['row'=8,'col'=4] {'row'}, use_global_device_ids=true, to_apply=%region_9.10 | all-reduce | flops 512 | bytes 4096 | tf_op jit(solution)/shard_map/pmax | solution.py:43
  77.2 0.2 exponential_reduce_fusion
  77.4 5.9 %psum.21 = f32[256]{0:T(256)S(1)} all-reduce(f32[256]{0:T(256)S(1)} %get-tuple-element.46), channel_id=1, replica_groups=mesh['row'=8,'col'=4] {'col'}, use_global_device_ids=true, to_apply=%region_5.6 | all-reduce | flops 256 | bytes 2048 | tf_op jit(solution)/shard_map/psum | solution.py:54
  83.3 17.1 %psum.22 = f32[512]{0:T(512)S(1)} all-reduce(f32[512]{0:T(512)S(1)} %get-tuple-element.45), channel_id=1, replica_groups=mesh['row'=8,'col'=4] {'row'}, use_global_device_ids=true, to_apply=%region_11.12 | all-reduce | flops 512 | bytes 4096 | tf_op jit(solution)/shard_map/psum | solution.py:55
  100.4 1.2 convolution_multiply_fusion.1
  101.7 0.0 reduce-scatter.3.cloned.1.call-update
  101.7 0.0 reduce-scatter.5.cloned.1.call-start
  101.7 1.5 convolution_multiply_fusion
  103.2 0.0 reduce-scatter.5.cloned.1.call-update
  103.2 18.0 %reduce-scatter.3.cloned.1.call-done = f32[64,512]{1,0:T(8,128)} async-done(((f32[256,512]{1,0:T(8,128)}), f32[64,512]{1,0:T(8,128)}) %reduce-scatter.3.cloned.1.call-update) | async-done | bytes 131088 | tf_op jit(solution)/shard_map/reduce_scatter | solution.py:94
  121.2 68.0 %reduce-scatter.5.cloned.1.call-done = f32[64,512]{1,0:T(8,128)} async-done(((f32[512,512]{1,0:T(8,128)}), f32[64,512]{1,0:T(8,128)}) %reduce-scatter.5.cloned.1.call-update) | async-done | bytes 131088 | tf_op jit(solution)/shard_map/reduce_scatter | solution.py:91
  189.2 0.0 copy-start.2
  189.2 0.0 copy-start.3
  189.2 1.3 multiply_reduce_fusion
  190.5 0.7 subtract_reduce_fusion
  192.5 39.9 %psum.23 = f32[]{:T(128)} all-reduce(f32[]{:T(128)S(6)} %add.61), channel_id=1, replica_groups=mesh['row'=8,'col'=4] {'row','col'}, use_global_device_ids=true, to_apply=%region_13.14 | all-reduce | flops 1 | bytes 8 | tf_op jit(solution)/shard_map/psum | solution.py:65
  233.0 0.0 copy-done.2
  233.0 0.0 copy-done.3
  233.0 0.8 subtract_divide_fusion
  (5 shorter events, 0.0 us)
Async XLA Ops:
  7.2 1.7 copy-start.1
  7.2 114.1 %reduce-scatter.3.cloned.1.call-start = ((), (), s32[]{:S(2)}) async-start(), calls=%async_computation.2 | async-start | bytes 655360 | tf_op jit(solution)/shard_map/reduce_scatter | solution.py:94
  8.9 33.2 %copy-start = (bf16[64,512]{1,0:T(8,128)(2,1)S(1)}, bf16[64,512]{1,0:T(8,128)(2,1)}, u32[]{:S(2)}) copy-start(bf16[64,512]{1,0:T(8,128)(2,1)} %param.3) | copy-start | bytes 196612
  101.7 87.6 %reduce-scatter.5.cloned.1.call-start = ((), (), s32[]{:S(2)}) async-start(), calls=%async_computation.3 | async-start | bytes 1179648 | tf_op jit(solution)/shard_map/reduce_scatter | solution.py:91
  189.2 43.8 %copy-start.2 = (f32[64,512]{1,0:T(8,128)S(1)}, f32[64,512]{1,0:T(8,128)}, u32[]{:S(2)}) copy-start(f32[64,512]{1,0:T(8,128)} %reduce-scatter.3.cloned.1.call-done) | copy-start | bytes 393220
  189.2 43.8 %copy-start.3 = (f32[64,512]{1,0:T(8,128)S(1)}, f32[64,512]{1,0:T(8,128)}, u32[]{:S(2)}) copy-start(f32[64,512]{1,0:T(8,128)} %reduce-scatter.5.cloned.1.call-done) | copy-start | bytes 393220
Sparse Core Ops, SparseCore 0:
  101.8 19.4 reduce-scatter.2
  124.7 64.5 reduce-scatter.4
where the time goes:
time: 242 us
  blocking collectives  130 us (54%)
  waiting for transfers between devices  86.1 us (36%)
  between operations  17.8 us (7%)
  other arithmetic  4.32 us (2%)
  matrix products  3.08 us (1%)
    reduce_scatter x1, waiting for transfers between devices, on_device(): lax.psum_scatter(txt_terms.reshape(columns, img_tile.shape[1]), 'row', sc...  68 us
    psum x1, blocking collectives, on_device(): overall = lax.psum(partial_value, ('row', 'col'))  39.9 us
    all_gather x1, blocking collectives, on_device(): txt_tile = lax.all_gather(txt_own, 'row', axis=0, tiled=True)  33.2 us
    pmax x1, blocking collectives, on_device(): col_peak = lax.pmax(col_peak.reshape(-1), 'row')  21.5 us
    reduce_scatter x1, waiting for transfers between devices, on_device(): lax.psum_scatter(img_terms, 'col', scatter_dimension=0, tiled=True)  18 us
    psum x1, blocking collectives, on_device(): col_sum = lax.psum(col_sum.reshape(-1), 'row')  17.1 us
    pmax x1, blocking collectives, on_device(): row_peak = lax.pmax(row_peak, 'col')  7.09 us
    psum x1, blocking collectives, on_device(): row_sum = lax.psum(row_sum, 'col')  5.91 us
  transfers between devices with their start and end apart: 2, of which 2 were waited for; matrix products, arithmetic and copies ran while one was open for 1% of the time, Pallas kernels for 0%

commit v1 on v0

--- a/solution.py
+++ b/solution.py
@@ -21,7 +21,12 @@
     img_own = unit_image.astype(jnp.bfloat16)
     txt_own = unit_text.astype(jnp.bfloat16)
     img_tile = lax.all_gather(img_own, "col", axis=0, tiled=True)
-    txt_tile = lax.all_gather(txt_own, "row", axis=0, tiled=True)
+    ring = [txt_own]
+    for hop in range(7):
+        ring.append(lax.ppermute(ring[-1], "row", [(dev, (dev + 1) % 8) for dev in range(8)]))
+    txt_tile = jnp.roll(
+        jnp.concatenate(ring[::-1], axis=0), (lax.axis_index("row") + 1) * ring[0].shape[0], axis=0
+    )
     columns = txt_tile.shape[0]
     block_cols = min(512, columns)
     block_count = columns // block_cols

time: 242 us -> 253 us (1.045)
  waiting for transfers between devices: 86.1 us -> 127 us
  blocking collectives: 130 us -> 97 us
  starting transfers between devices: 0.08 us -> 3.14 us
    ppermute x0 -> x7, waiting for transfers between devices: none -> 40.4 us  [on_device(): lax.ppermute(ring[-1], 'row', [(dev, (dev + 1) % 8) for dev in range(8)])]
    all_gather x1 -> x0, blocking collectives: 33.2 us -> none  [on_device(): txt_tile = lax.all_gather(txt_own, 'row', axis=0, tiled=True)]
    ppermute x0 -> x7, starting transfers between devices: none -> 3.06 us  [on_device(): lax.ppermute(ring[-1], 'row', [(dev, (dev + 1) % 8) for dev in range(8)])]
  transfers between devices with their start and end apart: 2 -> 9, of which waited for: 2 -> 9; matrix products, arithmetic and copies ran while one was open for 1% -> 1% of each run, Pallas kernels for 0% -> 0%
where the time goes in v1:
time: 253 us; the launch traced here: 252 us
  waiting for transfers between devices  127 us (50%)
  blocking collectives  97 us (38%)
  between operations  18 us (7%)
  other arithmetic  4.49 us (2%)
  starting transfers between devices  3.14 us (1%)
  matrix products  3.09 us (1%)
    reduce_scatter x1, waiting for transfers between devices, on_device(): lax.psum_scatter(txt_terms.reshape(columns, img_tile.shape[1]), 'row', sc...  68 us
    ppermute x7, waiting for transfers between devices, on_device(): lax.ppermute(ring[-1], 'row', [(dev, (dev + 1) % 8) for dev in range(8)])  40.4 us
    psum x1, blocking collectives, on_device(): overall = lax.psum(partial_value, ('row', 'col'))  39.9 us
    pmax x1, blocking collectives, on_device(): col_peak = lax.pmax(col_peak.reshape(-1), 'row')  21.8 us
    reduce_scatter x1, waiting for transfers between devices, on_device(): lax.psum_scatter(img_terms, 'col', scatter_dimension=0, tiled=True)  18.1 us
    psum x1, blocking collectives, on_device(): col_sum = lax.psum(col_sum.reshape(-1), 'row')  17.1 us
    pmax x1, blocking collectives, on_device(): row_peak = lax.pmax(row_peak, 'col')  6.23 us
    all_gather x1, blocking collectives, on_device(): img_tile = lax.all_gather(img_own, 'col', axis=0, tiled=True)  6.05 us
  transfers between devices with their start and end apart: 9, of which 9 were waited for; matrix products, arithmetic and copies ran while one was open for 1% of the time, Pallas kernels for 0%

profile of v1, /device:TPU:0, one launch (start us, length us, event | category | flops | bytes accessed | tf_op | source)
XLA Modules:
  0.0 252.4 jit_solution(3557928599187487725)
XLA Ops:
  7.2 0.0 copy-start
  7.2 0.0 reduce-scatter.3.cloned.1.call-start
  7.2 1.0 fusion.3
  8.2 0.0 copy-done
  8.2 0.0 copy-start.1
  8.2 0.1 fusion.10
  8.3 3.0 %collective-permute-start = (bf16[64,512]{1,0:T(8,128)(2,1)S(1)}, bf16[64,512]{1,0:T(8,128)(2,1)S(1)}, u32[]{:S(2)}, u32[]{:S(2)}) collective-permute-start(bf16[64,512]{1,0:T(8,128)(2,1)S(1)} %fusion.10), channel_id=1, source_target_pairs={{0,4},{4,8},{8,12},{12,16},{16,20},{20,24},{24,28},{28,0},{1,5},{5... | collective-permute-start | bytes 196616 | tf_op jit(solution)/shard_map/ppermute | solution.py:26
  11.4 5.3 %collective-permute-done = bf16[64,512]{1,0:T(8,128)(2,1)S(1)} collective-permute-done((bf16[64,512]{1,0:T(8,128)(2,1)S(1)}, bf16[64,512]{1,0:T(8,128)(2,1)S(1)}, u32[]{:S(2)}, u32[]{:S(2)}) %collective-permute-start) | collective-permute-done | bytes 65568 | tf_op jit(solution)/shard_map/ppermute | solution.py:26
  16.7 0.0 collective-permute-start.1
  16.7 7.0 %collective-permute-done.1 = bf16[64,512]{1,0:T(8,128)(2,1)S(1)} collective-permute-done((bf16[64,512]{1,0:T(8,128)(2,1)S(1)}, bf16[64,512]{1,0:T(8,128)(2,1)S(1)}, u32[]{:S(2)}, u32[]{:S(2)}) %collective-permute-start.1) | collective-permute-done | bytes 65568 | tf_op jit(solution)/shard_map/ppermute | solution.py:26
  23.6 0.0 collective-permute-start.2
  23.6 7.0 %collective-permute-done.2 = bf16[64,512]{1,0:T(8,128)(2,1)S(1)} collective-permute-done((bf16[64,512]{1,0:T(8,128)(2,1)S(1)}, bf16[64,512]{1,0:T(8,128)(2,1)S(1)}, u32[]{:S(2)}, u32[]{:S(2)}) %collective-permute-start.2) | collective-permute-done | bytes 65568 | tf_op jit(solution)/shard_map/ppermute | solution.py:26
  30.6 0.0 collective-permute-start.3
  30.6 0.0 copy-done.1
  30.6 0.1 fusion.2
  30.7 6.8 %collective-permute-done.3 = bf16[64,512]{1,0:T(8,128)(2,1)S(1)} collective-permute-done((bf16[64,512]{1,0:T(8,128)(2,1)S(1)}, bf16[64,512]{1,0:T(8,128)(2,1)S(1)}, u32[]{:S(2)}, u32[]{:S(2)}) %collective-permute-start.3) | collective-permute-done | bytes 65568 | tf_op jit(solution)/shard_map/ppermute | solution.py:26
  37.5 0.0 collective-permute-start.4
  37.6 7.3 %collective-permute-done.4 = bf16[64,512]{1,0:T(8,128)(2,1)S(1)} collective-permute-done((bf16[64,512]{1,0:T(8,128)(2,1)S(1)}, bf16[64,512]{1,0:T(8,128)(2,1)S(1)}, u32[]{:S(2)}, u32[]{:S(2)}) %collective-permute-start.4) | collective-permute-done | bytes 65568 | tf_op jit(solution)/shard_map/ppermute | solution.py:26
  44.8 0.0 collective-permute-start.5
  44.8 0.1 fusion.9
  45.6 6.2 %collective-permute-done.5 = bf16[64,512]{1,0:T(8,128)(2,1)S(1)} collective-permute-done((bf16[64,512]{1,0:T(8,128)(2,1)S(1)}, bf16[64,512]{1,0:T(8,128)(2,1)S(1)}, u32[]{:S(2)}, u32[]{:S(2)}) %collective-permute-start.5) | collective-permute-done | bytes 65568 | tf_op jit(solution)/shard_map/ppermute | solution.py:26
  51.8 0.0 collective-permute-start.6
  51.8 6.0 %all_gather.3 = bf16[256,512]{1,0:T(8,128)(2,1)S(1)} all-gather(bf16[64,512]{1,0:T(8,128)(2,1)S(1)} %fusion.9), channel_id=1, replica_groups=mesh['row'=8,'col'=4] {'col'}, dimensions={0}, use_global_device_ids=true | all-gather | bytes 327680 | tf_op jit(solution)/shard_map/all_gather | solution.py:23
  57.9 0.9 collective-permute-done.6
  58.9 0.1 constant_dynamic-update-slice_fusion.8
  59.1 0.1 constant_dynamic-update-slice_fusion
  59.1 0.4 fusion.11
  59.6 6.2 %pmax.14 = f32[256]{0:T(256)S(1)} all-reduce(f32[256]{0:T(256)S(1)} %broadcast_maximum_fusion), channel_id=1, replica_groups=mesh['row'=8,'col'=4] {'col'}, use_global_device_ids=true, to_apply=%region_3.4 | all-reduce | flops 256 | bytes 2048 | tf_op jit(solution)/shard_map/pmax | solution.py:47
  65.8 21.8 %pmax.15 = f32[512]{0:T(512)S(1)} all-reduce(f32[512]{0:T(512)S(1)} %get-tuple-element.47), channel_id=1, replica_groups=mesh['row'=8,'col'=4] {'row'}, use_global_device_ids=true, to_apply=%region_9.10 | all-reduce | flops 512 | bytes 4096 | tf_op jit(solution)/shard_map/pmax | solution.py:48
  87.6 0.2 exponential_reduce_fusion
  87.9 5.9 %psum.21 = f32[256]{0:T(256)S(1)} all-reduce(f32[256]{0:T(256)S(1)} %get-tuple-element.46), channel_id=1, replica_groups=mesh['row'=8,'col'=4] {'col'}, use_global_device_ids=true, to_apply=%region_5.6 | all-reduce | flops 256 | bytes 2048 | tf_op jit(solution)/shard_map/psum | solution.py:59
  93.8 17.1 %psum.22 = f32[512]{0:T(512)S(1)} all-reduce(f32[512]{0:T(512)S(1)} %get-tuple-element.45), channel_id=1, replica_groups=mesh['row'=8,'col'=4] {'row'}, use_global_device_ids=true, to_apply=%region_11.12 | all-reduce | flops 512 | bytes 4096 | tf_op jit(solution)/shard_map/psum | solution.py:60
  110.9 1.2 convolution_multiply_fusion.1
  112.1 0.0 reduce-scatter.3.cloned.1.call-update
  112.1 0.0 reduce-scatter.5.cloned.1.call-start
  112.2 1.5 convolution_multiply_fusion
  113.6 0.0 reduce-scatter.5.cloned.1.call-update
  113.6 18.1 %reduce-scatter.3.cloned.1.call-done = f32[64,512]{1,0:T(8,128)} async-done(((f32[256,512]{1,0:T(8,128)}), f32[64,512]{1,0:T(8,128)}) %reduce-scatter.3.cloned.1.call-update) | async-done | bytes 131088 | tf_op jit(solution)/shard_map/reduce_scatter | solution.py:99
  131.7 68.0 %reduce-scatter.5.cloned.1.call-done = f32[64,512]{1,0:T(8,128)} async-done(((f32[512,512]{1,0:T(8,128)}), f32[64,512]{1,0:T(8,128)}) %reduce-scatter.5.cloned.1.call-update) | async-done | bytes 131088 | tf_op jit(solution)/shard_map/reduce_scatter | solution.py:96
  199.7 0.0 copy-start.2
  199.7 0.0 copy-start.3
  199.7 1.3 multiply_reduce_fusion
  201.0 0.7 subtract_reduce_fusion
  203.0 39.9 %psum.23 = f32[]{:T(128)} all-reduce(f32[]{:T(128)S(6)} %add.77), channel_id=1, replica_groups=mesh['row'=8,'col'=4] {'row','col'}, use_global_device_ids=true, to_apply=%region_13.14 | all-reduce | flops 1 | bytes 8 | tf_op jit(solution)/shard_map/psum | solution.py:70
  243.5 0.0 copy-done.2
  243.5 0.0 copy-done.3
  243.5 0.8 subtract_divide_fusion
  (19 shorter events, 0.1 us)
Async XLA Ops:
  7.2 1.0 copy-start
  7.2 124.5 %reduce-scatter.3.cloned.1.call-start = ((), (), s32[]{:S(2)}) async-start(), calls=%async_computation.2 | async-start | bytes 655360 | tf_op jit(solution)/shard_map/reduce_scatter | solution.py:99
  8.2 22.4 %copy-start.1 = (bf16[64,512]{1,0:T(8,128)(2,1)S(1)}, bf16[64,512]{1,0:T(8,128)(2,1)}, u32[]{:S(2)}) copy-start(bf16[64,512]{1,0:T(8,128)(2,1)} %param.3) | copy-start | bytes 196612
  8.3 8.3 %collective-permute-start = (bf16[64,512]{1,0:T(8,128)(2,1)S(1)}, bf16[64,512]{1,0:T(8,128)(2,1)S(1)}, u32[]{:S(2)}, u32[]{:S(2)}) collective-permute-start(bf16[64,512]{1,0:T(8,128)(2,1)S(1)} %fusion.10), channel_id=1, source_target_pairs={{0,4},{4,8},{8,12},{12,16},{16,20},{20,24},{24,28},{28,0},{1,5},{5... | collective-permute-start | bytes 196616 | tf_op jit(solution)/shard_map/ppermute | solution.py:26
  16.7 7.0 %collective-permute-start.1 = (bf16[64,512]{1,0:T(8,128)(2,1)S(1)}, bf16[64,512]{1,0:T(8,128)(2,1)S(1)}, u32[]{:S(2)}, u32[]{:S(2)}) collective-permute-start(bf16[64,512]{1,0:T(8,128)(2,1)S(1)} %collective-permute-done), channel_id=1, source_target_pairs={{0,4},{4,8},{8,12},{12,16},{16,20},{20,24},{24,28},{28,0},{1,5},{5... | collective-permute-start | bytes 196616 | tf_op jit(solution)/shard_map/ppermute | solution.py:26
  23.6 7.0 %collective-permute-start.2 = (bf16[64,512]{1,0:T(8,128)(2,1)S(1)}, bf16[64,512]{1,0:T(8,128)(2,1)S(1)}, u32[]{:S(2)}, u32[]{:S(2)}) collective-permute-start(bf16[64,512]{1,0:T(8,128)(2,1)S(1)} %collective-permute-done.1), channel_id=1, source_target_pairs={{0,4},{4,8},{8,12},{12,16},{16,20},{20,24},{24,28},{28,0},{1,5},{5... | collective-permute-start | bytes 196616 | tf_op jit(solution)/shard_map/ppermute | solution.py:26
  30.6 7.0 %collective-permute-start.3 = (bf16[64,512]{1,0:T(8,128)(2,1)S(1)}, bf16[64,512]{1,0:T(8,128)(2,1)S(1)}, u32[]{:S(2)}, u32[]{:S(2)}) collective-permute-start(bf16[64,512]{1,0:T(8,128)(2,1)S(1)} %collective-permute-done.2), channel_id=1, source_target_pairs={{0,4},{4,8},{8,12},{12,16},{16,20},{20,24},{24,28},{28,0},{1,5},{5... | collective-permute-start | bytes 196616 | tf_op jit(solution)/shard_map/ppermute | solution.py:26
  37.5 7.3 %collective-permute-start.4 = (bf16[64,512]{1,0:T(8,128)(2,1)S(1)}, bf16[64,512]{1,0:T(8,128)(2,1)S(1)}, u32[]{:S(2)}, u32[]{:S(2)}) collective-permute-start(bf16[64,512]{1,0:T(8,128)(2,1)S(1)} %collective-permute-done.3), channel_id=1, source_target_pairs={{0,4},{4,8},{8,12},{12,16},{16,20},{20,24},{24,28},{28,0},{1,5},{5... | collective-permute-start | bytes 196616 | tf_op jit(solution)/shard_map/ppermute | solution.py:26
  44.8 7.0 %collective-permute-start.5 = (bf16[64,512]{1,0:T(8,128)(2,1)S(1)}, bf16[64,512]{1,0:T(8,128)(2,1)S(1)}, u32[]{:S(2)}, u32[]{:S(2)}) collective-permute-start(bf16[64,512]{1,0:T(8,128)(2,1)S(1)} %collective-permute-done.4), channel_id=1, source_target_pairs={{0,4},{4,8},{8,12},{12,16},{16,20},{20,24},{24,28},{28,0},{1,5},{5... | collective-permute-start | bytes 196616 | tf_op jit(solution)/shard_map/ppermute | solution.py:26
  51.8 7.0 %collective-permute-start.6 = (bf16[64,512]{1,0:T(8,128)(2,1)S(1)}, bf16[64,512]{1,0:T(8,128)(2,1)S(1)}, u32[]{:S(2)}, u32[]{:S(2)}) collective-permute-start(bf16[64,512]{1,0:T(8,128)(2,1)S(1)} %collective-permute-done.5), channel_id=1, source_target_pairs={{0,4},{4,8},{8,12},{12,16},{16,20},{20,24},{24,28},{28,0},{1,5},{5... | collective-permute-start | bytes 196616 | tf_op jit(solution)/shard_map/ppermute | solution.py:26
  112.1 87.6 %reduce-scatter.5.cloned.1.call-start = ((), (), s32[]{:S(2)}) async-start(), calls=%async_computation.3 | async-start | bytes 1179648 | tf_op jit(solution)/shard_map/reduce_scatter | solution.py:96
  199.7 43.8 %copy-start.2 = (f32[64,512]{1,0:T(8,128)S(1)}, f32[64,512]{1,0:T(8,128)}, u32[]{:S(2)}) copy-start(f32[64,512]{1,0:T(8,128)} %reduce-scatter.3.cloned.1.call-done) | copy-start | bytes 393220
  199.7 43.8 %copy-start.3 = (f32[64,512]{1,0:T(8,128)S(1)}, f32[64,512]{1,0:T(8,128)}, u32[]{:S(2)}) copy-start(f32[64,512]{1,0:T(8,128)} %reduce-scatter.5.cloned.1.call-done) | copy-start | bytes 393220
Sparse Core Ops, SparseCore 0:
  112.2 19.4 reduce-scatter.2
  135.1 64.5 reduce-scatter.4
